TPU v7x, 32 devices: a whole 2x2x4 slice. The times are simulated.
32 devices in a mesh: gx: 4 (over z), gy: 8 (over y, x, core).
Axes of the slice: x: 2, y: 2, z: 4, core: 2. Of those that a mesh axis runs over, the one named last changes fastest.
Arguments:
- die_basis: float32 [64, 256, 512], P('gx', 'gy'), may hold values from -0.078125 to 0.078125
- die_coeff: float32 [5, 64, 256], P(None, 'gx', 'gy'), may hold values from 0.2 to 5
- pkg_basis: float32 [1024, 64, 512], P(('gx', 'gy')), may hold values from -0.09375 to 0.09375
- send_blocks: int32 [32, 4, 4], P(('gx', 'gy')), may hold values from 0 to 31
- columns: int32 [5, 1024, 4], P(None, ('gx', 'gy')), may hold values from 0 to 47
- counts: int32 [5, 1024], P(None, ('gx', 'gy')), may hold values from 1 to 4
- pkg_blocks: float32 [5, 1024, 64, 256], P(None, ('gx', 'gy')), may hold values from -48 to 48
Outputs:
- reduced: float32 [5, 512, 512], replicated
Inputs may be any that keep to these rules, and one draw needn't show every extreme that they name: `columns`: indices below 32 name the partition's own blocks, the others its ghost blocks in the order of the statement.
All inputs are finite; a program needn't handle non-finite values.
Results may differ from a plain program's by a relative error of at most 0.0001.
Values sent between devices are 32-bit elements; how exact they have to be, the bound alone decides.
No kernel may reach another device: no remote copies, remote signals or barrier semaphores. Data moves between devices by JAX's collectives and lax.ppermute only.
A program may use at most 256 MiB of HBM per device.

v0:
```python
import jax
import jax.numpy as jnp
from jax import lax
from jax.sharding import PartitionSpec as P

highest = lax.Precision.HIGHEST


def from_behind(value, axis, steps):
    count = lax.axis_size(axis)
    leading, last = (max(0, -steps), min(count, count - steps))
    return lax.ppermute(value, axis, [(source, source + steps) for source in range(leading, last)])


def passed_along(value, axis, steps):
    count = lax.axis_size(axis)
    pairs = [(source, (source + steps) % count) for source in range(count)]
    return lax.ppermute(value, axis, pairs)


def weighted_gram(weights, field):
    width = field.shape[-1]
    flat = field.reshape(-1, width)
    scaled = weights.reshape(-1, 1) * flat
    return lax.dot_general(
        flat,
        scaled,
        (((0,), (0,)), ((), ())),
        precision=highest,
        preferred_element_type=jnp.float32,
    )


def die_terms(basis, coeff, next_x_row, next_y_col):
    next_x = jnp.concatenate([basis[1:], next_x_row], axis=0)
    next_y = jnp.concatenate([basis[:, 1:], next_y_col], axis=1)
    diff_x = basis - next_x
    diff_y = basis - next_y
    return jnp.stack(
        [
            weighted_gram(coeff[0], basis),
            weighted_gram(coeff[1], diff_x),
            weighted_gram(coeff[2], diff_y),
            weighted_gram(coeff[3], basis),
            weighted_gram(coeff[4], diff_x) + weighted_gram(coeff[4], diff_y),
        ]
    )


def package_terms(owned, table, columns, counts, blocks):
    row_count = owned.shape[0]
    block = owned.shape[1]
    width = owned.shape[2]
    entries = columns.shape[-1]
    results = []
    for term_idx in range(columns.shape[0]):
        picked = table[columns[term_idx]]
        live = (jnp.arange(entries, dtype=jnp.int32)[None, :] < counts[term_idx][:, None]).astype(
            jnp.float32
        )
        matrices = (
            blocks[term_idx].reshape(row_count, block, entries, block) * live[:, None, :, None]
        )
        image = jnp.einsum("rinj,rnjk->rik", matrices, picked, precision=highest)
        results.append(
            lax.dot_general(
                owned.reshape(-1, width),
                image.reshape(-1, width),
                (((0,), (0,)), ((), ())),
                precision=highest,
                preferred_element_type=jnp.float32,
            )
        )
    return jnp.stack(results)


def body(die_basis, die_coeff, pkg_basis, send_blocks, columns, counts, pkg_blocks):
    next_x_row = from_behind(die_basis[:1], "gx", -1)
    next_y_col = from_behind(die_basis[:, :1], "gy", -1)
    lists = send_blocks[0]
    from_lower_x = passed_along(pkg_basis[lists[0]], "gx", 1)
    from_upper_x = passed_along(pkg_basis[lists[1]], "gx", -1)
    from_lower_y = passed_along(pkg_basis[lists[2]], "gy", 1)
    from_upper_y = passed_along(pkg_basis[lists[3]], "gy", -1)
    table = jnp.concatenate(
        [pkg_basis, from_lower_x, from_upper_x, from_lower_y, from_upper_y], axis=0
    )
    partial_terms = die_terms(die_basis, die_coeff, next_x_row, next_y_col)
    partial_terms = partial_terms + package_terms(pkg_basis, table, columns, counts, pkg_blocks)
    return lax.psum(partial_terms, ("gx", "gy"))


def solution(mesh):
    placed = (
        P("gx", "gy", None),
        P(None, "gx", "gy"),
        P(("gx", "gy"), None, None),
        P(("gx", "gy"), None, None),
        P(None, ("gx", "gy"), None),
        P(None, ("gx", "gy")),
        P(None, ("gx", "gy"), None, None),
    )
    return jax.shard_map(body, mesh=mesh, in_specs=placed, out_specs=P(), check_vma=False)
```

profile of v0, /device:TPU:0, one launch (start us, length us, event | category | flops | bytes accessed | tf_op | source)
XLA Modules:
  0.0 460.3 jit_solution(5091545625883094443)
XLA Ops:
  30.8 4.9 %constant_dynamic-update-slice_fusion.4 = f32[48,64,512]{2,1,0:T(8,128)} fusion(f32[32,64,512]{2,1,0:T(8,128)} %param.9), kind=kLoop, calls=%fused_computation.81 | loop fusion | bytes 8388608
  36.1 7.9 %fusion.120 = (f32[1,32,64,256]{3,2,1,0:T(8,128)S(1)}, f32[1,32,64,256]{3,2,1,0:T(8,128)}, f32[1,32,64,256]{3,2,1,0:T(8,128)}, f32[1,32,64,256]{3,2,1,0:T(8,128)}, f32[1,32,64,256]{3,2,1,0:T(8,128)}) fusion(f32[5,32,64,256]{3,2,1,0:T(8,128)} %param.13), kind=kLoop, calls=%fused_computation.128 | loop fusion | bytes 20971520 | tf_op jit(solution)/shard_map/slice | solution.py:62
  44.0 5.1 %reshape_squeeze.22 = f32[32,64,4,64]{3,2,1,0:T(4,128)} reshape(f32[1,32,64,256]{3,2,1,0:T(8,128)} %get-tuple-element.7) | data formatting | bytes 4194304 | tf_op jit(solution)/shard_map/reshape;squeeze | solution.py:62
  49.3 5.1 %reshape_squeeze.10 = f32[32,64,4,64]{3,2,1,0:T(4,128)} reshape(f32[1,32,64,256]{3,2,1,0:T(8,128)} %get-tuple-element.8) | data formatting | bytes 4194304 | tf_op jit(solution)/shard_map/reshape;squeeze | solution.py:62
  54.3 5.1 %reshape_squeeze.23 = f32[32,64,4,64]{3,2,1,0:T(4,128)} reshape(f32[1,32,64,256]{3,2,1,0:T(8,128)} %get-tuple-element.6) | data formatting | bytes 4194304 | tf_op jit(solution)/shard_map/reshape;squeeze | solution.py:62
  59.8 5.1 %reshape_squeeze.24 = f32[32,64,4,64]{3,2,1,0:T(4,128)} reshape(f32[1,32,64,256]{3,2,1,0:T(8,128)} %get-tuple-element.9) | data formatting | bytes 4194304 | tf_op jit(solution)/shard_map/reshape;squeeze | solution.py:62
  110.8 12.9 %gather_fusion.5 = f32[128,64,512]{2,1,0:T(8,128)} fusion(f32[48,64,512]{2,1,0:T(8,128)} %constant_dynamic-update-slice_fusion, s32[1024]{0:T(1024)S(1)} %get-tuple-element.32), kind=kCustom, calls=%fused_computation.5 | custom fusion | bytes 33554944 | tf_op jit(solution)/shard_map/gather | solution.py:57
  123.7 12.7 %gather_fusion.4 = f32[128,64,512]{2,1,0:T(8,128)} fusion(f32[48,64,512]{2,1,0:T(8,128)} %constant_dynamic-update-slice_fusion, s32[1024]{0:T(1024)S(1)} %pad_clamp_fusion.4), kind=kCustom, calls=%fused_computation.4 | custom fusion | bytes 33554944 | tf_op jit(solution)/shard_map/gather | solution.py:57
  136.4 13.9 %fusion.18 = f32[32,64,512,1]{2,1,3,0:T(8,128)S(1)} fusion(f32[32,4,64,512]{3,2,1,0:T(8,128)} %bitcast.211, f32[32,64,4,64]{3,2,1,0:T(4,128)} %broadcast_multiply_fusion.4), kind=kOutput, calls=%fused_computation.27 | convolution fusion | flops 3221225472 | bytes 23068672 | tf_op jit(solution)/shard_map/rinj,rnjk->rik/dot_general | solution.py:64
  150.4 8.0 %fusion.65 = f32[5,512,512]{1,2,0:T(8,128)} fusion(f32[32,64,512]{2,1,0:T(8,128)S(1)} %copy-done.9, f32[32,64,512,1]{2,1,3,0:T(8,128)S(1)} %fusion.18), kind=kOutput, calls=%fused_computation.57 | convolution fusion | flops 6442450944 | bytes 9437184 | tf_op jit(solution)/shard_map/dot_general | solution.py:66
  158.3 12.7 %gather_fusion.6 = f32[128,64,512]{2,1,0:T(8,128)} fusion(f32[48,64,512]{2,1,0:T(8,128)} %constant_dynamic-update-slice_fusion, s32[1024]{0:T(1024)S(1)} %get-tuple-element.31), kind=kCustom, calls=%fused_computation.6 | custom fusion | bytes 33554944 | tf_op jit(solution)/shard_map/gather | solution.py:57
  171.0 12.7 %gather_fusion.7 = f32[128,64,512]{2,1,0:T(8,128)} fusion(f32[48,64,512]{2,1,0:T(8,128)} %constant_dynamic-update-slice_fusion, s32[1024]{0:T(1024)S(1)} %get-tuple-element.30), kind=kCustom, calls=%fused_computation.7 | custom fusion | bytes 33554944 | tf_op jit(solution)/shard_map/gather | solution.py:57
  183.7 12.9 %gather_fusion.8 = f32[128,64,512]{2,1,0:T(8,128)} fusion(f32[48,64,512]{2,1,0:T(8,128)} %constant_dynamic-update-slice_fusion, s32[1024]{0:T(1024)S(1)} %get-tuple-element.29), kind=kCustom, calls=%fused_computation.8 | custom fusion | bytes 33554944 | tf_op jit(solution)/shard_map/gather | solution.py:57
  196.5 16.1 %fusion.16 = f32[32,64,512,1]{2,1,3,0:T(8,128)} fusion(f32[32,4,64,512]{3,2,1,0:T(8,128)} %bitcast.206, f32[32,64,4,64]{3,2,1,0:T(4,128)} %broadcast_multiply_fusion.3), kind=kOutput, calls=%fused_computation.25 | convolution fusion | flops 3221225472 | bytes 23068672 | tf_op jit(solution)/shard_map/rinj,rnjk->rik/dot_general | solution.py:64
  212.6 10.4 %fusion.71 = f32[5,512,512]{1,2,0:T(8,128)} fusion(f32[5,512,512]{1,2,0:T(8,128)} %fusion.65, f32[32,64,512]{2,1,0:T(8,128)} %param.9, f32[32,64,512,1]{2,1,3,0:T(8,128)} %fusion.16), kind=kOutput, calls=%fused_computation.59 | convolution fusion | flops 6442450944 | bytes 9437184 | tf_op jit(solution)/shard_map/dot_general | solution.py:66
  223.0 12.0 %fusion.14 = f32[32,64,512,1]{2,1,3,0:T(8,128)} fusion(f32[32,4,64,512]{3,2,1,0:T(8,128)S(1)} %bitcast.210, f32[32,64,4,64]{3,2,1,0:T(4,128)S(1)} %copy-done.6), kind=kOutput, calls=%fused_computation.23 | convolution fusion | flops 3221225472 | bytes 23068672 | tf_op jit(solution)/shard_map/rinj,rnjk->rik/dot_general | solution.py:64
  235.1 10.4 %fusion.77 = f32[5,512,512]{1,2,0:T(8,128)} fusion(f32[5,512,512]{1,2,0:T(8,128)} %fusion.71, f32[32,64,512]{2,1,0:T(8,128)} %param.9, f32[32,64,512,1]{2,1,3,0:T(8,128)} %fusion.14), kind=kOutput, calls=%fused_computation.61 | convolution fusion | flops 6442450944 | bytes 9437184 | tf_op jit(solution)/shard_map/dot_general | solution.py:66
  245.5 14.7 %fusion.12 = f32[32,64,512,1]{2,1,3,0:T(8,128)} fusion(f32[32,4,64,512]{3,2,1,0:T(8,128)} %bitcast.207, f32[32,64,4,64]{3,2,1,0:T(4,128)S(1)} %copy-done.8), kind=kOutput, calls=%fused_computation.21 | convolution fusion | flops 3221225472 | bytes 23068672 | tf_op jit(solution)/shard_map/rinj,rnjk->rik/dot_general | solution.py:64
  260.2 10.6 %fusion.83 = f32[5,512,512]{1,2,0:T(8,128)} fusion(f32[5,512,512]{1,2,0:T(8,128)} %fusion.77, f32[32,64,512]{2,1,0:T(8,128)} %param.9, f32[32,64,512,1]{2,1,3,0:T(8,128)} %fusion.12), kind=kOutput, calls=%fused_computation.63 | convolution fusion | flops 6442450944 | bytes 9437184 | tf_op jit(solution)/shard_map/dot_general | solution.py:66
  270.8 11.8 %fusion.10 = f32[32,64,512,1]{2,1,3,0:T(8,128)} fusion(f32[32,4,64,512]{3,2,1,0:T(8,128)S(1)} %bitcast.205, f32[32,64,4,64]{3,2,1,0:T(4,128)S(1)} %copy-done.7), kind=kOutput, calls=%fused_computation.19 | convolution fusion | flops 3221225472 | bytes 23068672 | tf_op jit(solution)/shard_map/rinj,rnjk->rik/dot_general | solution.py:64
  282.6 10.2 %fusion.89 = f32[5,512,512]{1,2,0:T(8,128)} fusion(f32[5,512,512]{1,2,0:T(8,128)} %fusion.83, f32[32,64,512]{2,1,0:T(8,128)} %param.9, f32[32,64,512,1]{2,1,3,0:T(8,128)} %fusion.10), kind=kOutput, calls=%fused_computation.65 | convolution fusion | flops 6442450944 | bytes 9437184 | tf_op jit(solution)/shard_map/dot_general | solution.py:66
  292.9 7.9 %add.108 = f32[5,512,512]{1,2,0:T(8,128)} add(f32[5,512,512]{1,2,0:T(8,128)} %copy-done.10, f32[5,512,512]{1,2,0:T(8,128)} %fusion.89) | non-fusion elementwise | flops 1310720 | bytes 15728640 | tf_op jit(solution)/shard_map/add | solution.py:89
  300.8 146.3 %all-reduce.2.cloned.1.call-done = f32[5,512,512]{1,2,0:T(8,128)} async-done(((f32[5,512,512]{1,2,0:T(8,128)}), f32[5,512,512]{1,2,0:T(8,128)}) %all-reduce.2.cloned.1.call-update) | async-done | bytes 5242896 | tf_op jit(solution)/shard_map/psum | solution.py:90
  447.1 5.9 %copy.27 = f32[5,512,512]{2,1,0:T(8,128)} copy(f32[5,512,512]{1,2,0:T(8,128)} %all-reduce.2.cloned.1.call-done) | data formatting | bytes 10485760 | tf_op jit(solution)/shard_map/psum | solution.py:90
  (108 shorter events, 71.1 us)
Async XLA Ops:
  6.5 22.9 %copy-start = (f32[16,32,512]{2,1,0:T(8,128)S(1)}, f32[16,32,512]{2,1,0:T(8,128)}, u32[]{:S(2)}) copy-start(f32[16,32,512]{2,1,0:T(8,128)} %param.7) | copy-start | bytes 3145732
  6.5 440.6 %all-reduce.2.cloned.1.call-start = ((), (), s32[]{:S(2)}) async-start(), calls=%async_computation | async-start | bytes 10485760 | tf_op jit(solution)/shard_map/psum | solution.py:90
  11.0 92.4 %collective-permute-start.2 = (f32[4,64,512]{2,1,0:T(8,128)}, f32[4,64,512]{2,1,0:T(8,128)}, u32[]{:S(2)}, u32[]{:S(2)}) collective-permute-start(f32[4,64,512]{2,1,0:T(8,128)} %gather_fusion), channel_id=1, source_target_pairs={{0,8},{8,16},{16,24},{24,0},{1,9},{9,17},{17,25},{25,1},{2,10},{10... | collective-permute-start | bytes 1572872 | tf_op jit(solution)/shard_map/ppermute | solution.py:18
  17.6 87.6 %collective-permute-start.3 = (f32[4,64,512]{2,1,0:T(8,128)}, f32[4,64,512]{2,1,0:T(8,128)}, u32[]{:S(2)}, u32[]{:S(2)}) collective-permute-start(f32[4,64,512]{2,1,0:T(8,128)} %gather_fusion.1), channel_id=1, source_target_pairs={{0,24},{8,0},{16,8},{24,16},{1,25},{9,1},{17,9},{25,17},{2,26},{10... | collective-permute-start | bytes 1572872 | tf_op jit(solution)/shard_map/ppermute | solution.py:18
  23.2 83.9 %collective-permute-start.4 = (f32[4,64,512]{2,1,0:T(8,128)}, f32[4,64,512]{2,1,0:T(8,128)}, u32[]{:S(2)}, u32[]{:S(2)}) collective-permute-start(f32[4,64,512]{2,1,0:T(8,128)} %gather_fusion.2), channel_id=1, source_target_pairs={{0,1},{1,2},{2,3},{3,4},{4,5},{5,6},{6,7},{7,0},{8,9},{9,10},{10,1... | collective-permute-start | bytes 1572872 | tf_op jit(solution)/shard_map/ppermute | solution.py:18
  26.8 82.2 %collective-permute-start.5 = (f32[4,64,512]{2,1,0:T(8,128)}, f32[4,64,512]{2,1,0:T(8,128)}, u32[]{:S(2)}, u32[]{:S(2)}) collective-permute-start(f32[4,64,512]{2,1,0:T(8,128)} %gather_fusion.3), channel_id=1, source_target_pairs={{0,7},{1,0},{2,1},{3,2},{4,3},{5,4},{6,5},{7,6},{8,15},{9,8},{10,9... | collective-permute-start | bytes 1572872 | tf_op jit(solution)/shard_map/ppermute | solution.py:18
  29.5 6.2 %copy-start.12 = (s32[5,32,4]{1,2,0:T(4,128)S(1)}, s32[5,32,4]{1,2,0:T(4,128)}, u32[]{:S(2)}) copy-start(s32[5,32,4]{1,2,0:T(4,128)} %param.11) | copy-start | bytes 7684
  29.5 6.6 %copy-start.13 = (s32[5,32]{1,0:T(8,128)S(1)}, s32[5,32]{1,0:T(8,128)}, u32[]{:S(2)}) copy-start(s32[5,32]{1,0:T(8,128)} %param.12) | copy-start | bytes 1924
  29.5 56.2 %collective-permute-start.1 = (f32[16,1,512]{2,1,0:T(1,128)S(1)}, f32[16,1,512]{2,1,0:T(1,128)S(1)}, u32[]{:S(2)}, u32[]{:S(2)}) collective-permute-start(f32[16,1,512]{2,1,0:T(1,128)S(1)} %slice.94), channel_id=1, source_target_pairs={{1,0},{2,1},{3,2},{4,3},{5,4},{6,5},{7,6},{9,8},{10,9},{11,10},{12... | collective-permute-start | bytes 98312 | tf_op jit(solution)/shard_map/ppermute | solution.py:12
  64.9 3.6 copy-start.11
  73.5 3.0 copy-start.1
  85.7 6.7 %collective-permute-start = (f32[1,32,512]{2,1,0:T(8,128)S(1)}, f32[1,32,512]{2,1,0:T(8,128)S(1)}, u32[]{:S(2)}, u32[]{:S(2)}) collective-permute-start(f32[1,32,512]{2,1,0:T(8,128)S(1)} %slice.91), channel_id=1, source_target_pairs={{8,0},{16,8},{24,16},{9,1},{17,9},{25,17},{10,2},{18,10},{26,18},{... | collective-permute-start | bytes 196616 | tf_op jit(solution)/shard_map/ppermute | solution.py:12
  136.4 14.0 %copy-start.9 = (f32[32,64,512]{2,1,0:T(8,128)S(1)}, f32[32,64,512]{2,1,0:T(8,128)}, u32[]{:S(2)}) copy-start(f32[32,64,512]{2,1,0:T(8,128)} %param.9) | copy-start | bytes 12582916
  196.5 26.5 %slice-start.4 = ((s8[16777216]{0:T(1024)(128)(4,1)}), s8[4194304]{0:T(1024)(128)(4,1)S(1)}, s32[]{:S(2)}) async-start(s8[16777216]{0:T(1024)(128)(4,1)} %bitcast.208), calls=%async_computation.5 | async-start | bytes 8388608
  196.5 26.5 %slice-start.5 = ((s8[16777216]{0:T(1024)(128)(4,1)}), s8[4194304]{0:T(1024)(128)(4,1)S(1)}, s32[]{:S(2)}) async-start(s8[16777216]{0:T(1024)(128)(4,1)} %bitcast.208), calls=%async_computation.6 | async-start | bytes 8388608
  196.5 26.5 %slice-start.6 = ((s8[16777216]{0:T(1024)(128)(4,1)}), s8[4194304]{0:T(1024)(128)(4,1)S(1)}, s32[]{:S(2)}) async-start(s8[16777216]{0:T(1024)(128)(4,1)} %bitcast.208), calls=%async_computation.7 | async-start | bytes 8388608
  212.6 10.4 %slice-start.7 = ((s8[16777216]{0:T(1024)(128)(4,1)}), s8[4194304]{0:T(1024)(128)(4,1)S(1)}, s32[]{:S(2)}) async-start(s8[16777216]{0:T(1024)(128)(4,1)} %bitcast.208), calls=%async_computation.8 | async-start | bytes 8388608
  212.6 10.4 %copy-start.6 = (f32[32,64,4,64]{3,2,1,0:T(4,128)S(1)}, f32[32,64,4,64]{3,2,1,0:T(4,128)}, u32[]{:S(2)}) copy-start(f32[32,64,4,64]{3,2,1,0:T(4,128)} %broadcast_multiply_fusion.2) | copy-start | bytes 6291460
  235.1 10.4 %copy-start.8 = (f32[32,64,4,64]{3,2,1,0:T(4,128)S(1)}, f32[32,64,4,64]{3,2,1,0:T(4,128)}, u32[]{:S(2)}) copy-start(f32[32,64,4,64]{3,2,1,0:T(4,128)} %broadcast_multiply_fusion.1) | copy-start | bytes 6291460
  245.5 25.3 %slice-start = ((s8[16777216]{0:T(1024)(128)(4,1)}), s8[4194304]{0:T(1024)(128)(4,1)S(1)}, s32[]{:S(2)}) async-start(s8[16777216]{0:T(1024)(128)(4,1)} %bitcast.203), calls=%async_computation.1 | async-start | bytes 8388608
  245.5 25.3 %slice-start.1 = ((s8[16777216]{0:T(1024)(128)(4,1)}), s8[4194304]{0:T(1024)(128)(4,1)S(1)}, s32[]{:S(2)}) async-start(s8[16777216]{0:T(1024)(128)(4,1)} %bitcast.203), calls=%async_computation.2 | async-start | bytes 8388608
  245.5 25.3 %slice-start.2 = ((s8[16777216]{0:T(1024)(128)(4,1)}), s8[4194304]{0:T(1024)(128)(4,1)S(1)}, s32[]{:S(2)}) async-start(s8[16777216]{0:T(1024)(128)(4,1)} %bitcast.203), calls=%async_computation.3 | async-start | bytes 8388608
  260.2 10.6 %slice-start.3 = ((s8[16777216]{0:T(1024)(128)(4,1)}), s8[4194304]{0:T(1024)(128)(4,1)S(1)}, s32[]{:S(2)}) async-start(s8[16777216]{0:T(1024)(128)(4,1)} %bitcast.203), calls=%async_computation.4 | async-start | bytes 8388608
  260.2 10.6 %copy-start.7 = (f32[32,64,4,64]{3,2,1,0:T(4,128)S(1)}, f32[32,64,4,64]{3,2,1,0:T(4,128)}, u32[]{:S(2)}) copy-start(f32[32,64,4,64]{3,2,1,0:T(4,128)} %broadcast_multiply_fusion) | copy-start | bytes 6291460
  (5 other events, 13.4 us)
Sparse Core Ops, SparseCore 0:
  301.0 146.1 all-reduce.1
where the time goes:
time: 468 us; the launch traced here: 460 us
  waiting for transfers between devices  149 us (32%)
  local copies, waits for them, and re-layouts  132 us (28%)
  matrix products  131 us (28%)
  other arithmetic  23.7 us (5%)
  between operations  14.2 us (3%)
  starting transfers between devices  10.5 us (2%)
    psum x1, waiting for transfers between devices, body(): return lax.psum(partial_terms, ('gx', 'gy'))  146 us
    dot_general x5, matrix products, package_terms(): image = jnp.einsum('rinj,rnjk->rik', matrices, picked, precision=highest)  68.6 us
    gather x5, local copies, waits for them, and re-layouts, package_terms(): picked = table[columns[term_idx]]  63.7 us
    dot_general x5, matrix products, package_terms(): lax.dot_general(owned.reshape(-1, width), image.reshape(-1, width), (((0,...  49.6 us
    another operation x5, local copies, waits for them, and re-layouts, package_terms(): blocks[term_idx].reshape(row_count, block, entries, block)  23.8 us
    mul x5, other arithmetic, package_terms(): blocks[term_idx].reshape(row_count, block, entries, block)  14.7 us
    unnamed x48, local copies, waits for them, and re-layouts  13 us
    dot_general x6, matrix products, weighted_gram(): lax.dot_general(flat, scaled, (((0,), (0,)), ((), ())), precision=highest...  12.7 us
  transfers between devices with their start and end apart: 7, of which 2 were waited for; matrix products, arithmetic and copies ran while one was open for 18% of the time, Pallas kernels for 0%

commit v1 on v0

--- a/solution.py
+++ b/solution.py
@@ -75,6 +75,11 @@
 
 
 def body(die_basis, die_coeff, pkg_basis, send_blocks, columns, counts, pkg_blocks):
+
+    def pipes_store(tile_in, link_axis):
+        f_next = jnp.sum(lax.all_gather(tile_in, link_axis), 0)
+        return f_next
+
     next_x_row = from_behind(die_basis[:1], "gx", -1)
     next_y_col = from_behind(die_basis[:, :1], "gy", -1)
     lists = send_blocks[0]
@@ -87,7 +92,7 @@
     )
     partial_terms = die_terms(die_basis, die_coeff, next_x_row, next_y_col)
     partial_terms = partial_terms + package_terms(pkg_basis, table, columns, counts, pkg_blocks)
-    return lax.psum(partial_terms, ("gx", "gy"))
+    return pipes_store(partial_terms, ("gx", "gy"))
 
 
 def solution(mesh):

time: 468 us -> 1210 us (2.59)
  waiting for transfers between devices: 149 us -> 840 us
  other arithmetic: 23.7 us -> 62.8 us
    all_gather x0 -> x1, waiting for transfers between devices: none -> 840 us  [pipes_store(): f_next = jnp.sum(lax.all_gather(tile_in, link_axis), 0)]
    psum x1 -> x0, waiting for transfers between devices: 146 us -> none  [body(): return lax.psum(partial_terms, ('gx', 'gy'))]
    reduce_sum x0 -> x1, other arithmetic: none -> 53.2 us  [pipes_store(): f_next = jnp.sum(lax.all_gather(tile_in, link_axis), 0)]
    mul x5 -> x0, other arithmetic: 14.7 us -> none  [package_terms(): blocks[term_idx].reshape(row_count, block, entries, block)]
  transfers between devices with their start and end apart: 7 -> 7, of which waited for: 2 -> 1; matrix products, arithmetic and copies ran while one was open for 18% -> 7% of each run, Pallas kernels for 0% -> 0%
where the time goes in v1:
time: 1210 us; the launch traced here: 1200 us
  waiting for transfers between devices  840 us (69%)
  matrix products  138 us (11%)
  local copies, waits for them, and re-layouts  132 us (11%)
  other arithmetic  62.8 us (5%)
  between operations  13.9 us (1%)
  starting transfers between devices  12.1 us (1%)
    all_gather x1, waiting for transfers between devices, pipes_store(): f_next = jnp.sum(lax.all_gather(tile_in, link_axis), 0)  840 us
    dot_general x5, matrix products, package_terms(): image = jnp.einsum('rinj,rnjk->rik', matrices, picked, precision=highest)  70.9 us
    gather x5, local copies, waits for them, and re-layouts, package_terms(): picked = table[columns[term_idx]]  63.6 us
    reduce_sum x1, other arithmetic, pipes_store(): f_next = jnp.sum(lax.all_gather(tile_in, link_axis), 0)  53.2 us
    dot_general x5, matrix products, package_terms(): lax.dot_general(owned.reshape(-1, width), image.reshape(-1, width), (((0,...  50.1 us
    another operation x5, local copies, waits for them, and re-layouts, package_terms(): blocks[term_idx].reshape(row_count, block, entries, block)  25.3 us
  transfers between devices with their start and end apart: 7, of which 1 were waited for; matrix products, arithmetic and copies ran while one was open for 7% of the time, Pallas kernels for 0%

profile of v1, /device:TPU:0, one launch (start us, length us, event | category | flops | bytes accessed | tf_op | source)
XLA Modules:
  0.0 1199.4 jit_solution(7505515507032009520)
XLA Ops:
  40.6 8.2 fusion.120
  53.5 5.1 reshape_squeeze.25
  58.6 5.1 reshape_squeeze.23
  68.7 5.1 reshape_squeeze.10
  73.8 5.1 reshape_squeeze.24
  100.2 12.9 %gather_fusion.8 = f32[128,64,512]{2,1,0:T(8,128)} fusion(f32[48,64,512]{2,1,0:T(8,128)} %constant_dynamic-update-slice_fusion, s32[1024]{0:T(1024)S(1)} %get-tuple-element.29), kind=kCustom, calls=%fused_computation.8 | custom fusion | bytes 33554944 | tf_op jit(solution)/shard_map/gather | solution.py:57
  113.0 12.7 %gather_fusion.7 = f32[128,64,512]{2,1,0:T(8,128)} fusion(f32[48,64,512]{2,1,0:T(8,128)} %constant_dynamic-update-slice_fusion, s32[1024]{0:T(1024)S(1)} %get-tuple-element.30), kind=kCustom, calls=%fused_computation.7 | custom fusion | bytes 33554944 | tf_op jit(solution)/shard_map/gather | solution.py:57
  125.7 12.7 %gather_fusion.6 = f32[128,64,512]{2,1,0:T(8,128)} fusion(f32[48,64,512]{2,1,0:T(8,128)} %constant_dynamic-update-slice_fusion, s32[1024]{0:T(1024)S(1)} %get-tuple-element.31), kind=kCustom, calls=%fused_computation.6 | custom fusion | bytes 33554944 | tf_op jit(solution)/shard_map/gather | solution.py:57
  138.4 12.7 %gather_fusion.5 = f32[128,64,512]{2,1,0:T(8,128)} fusion(f32[48,64,512]{2,1,0:T(8,128)} %constant_dynamic-update-slice_fusion, s32[1024]{0:T(1024)S(1)} %get-tuple-element.32), kind=kCustom, calls=%fused_computation.5 | custom fusion | bytes 33554944 | tf_op jit(solution)/shard_map/gather | solution.py:57
  151.1 12.8 %gather_fusion.4 = f32[128,64,512]{2,1,0:T(8,128)} fusion(f32[48,64,512]{2,1,0:T(8,128)} %constant_dynamic-update-slice_fusion, s32[1024]{0:T(1024)S(1)} %pad_clamp_fusion.4), kind=kCustom, calls=%fused_computation.4 | custom fusion | bytes 33554944 | tf_op jit(solution)/shard_map/gather | solution.py:57
  163.8 14.5 %fusion.14 = f32[32,64,512,1]{2,1,3,0:T(8,128)S(1)} fusion(f32[32,4,64,512]{3,2,1,0:T(8,128)} %bitcast.213, f32[32,64,4,64]{3,2,1,0:T(4,128)} %reshape_squeeze.10, f32[32,4]{1,0:T(8,128)S(1)} %get-tuple-element.33), kind=kOutput, calls=%fused_computation.28 | convolution fusion | flops 3221749760 | bytes 23069184 | tf_op jit(solution)/shard_map/rinj,rnjk->rik/dot_general | solution.py:64
  178.4 8.0 fusion.65
  186.4 15.3 %fusion.13 = f32[32,64,512,1]{2,1,3,0:T(8,128)} fusion(f32[32,4,64,512]{3,2,1,0:T(8,128)} %bitcast.212, f32[32,64,4,64]{3,2,1,0:T(4,128)S(1)} %copy-done.4, f32[32,4]{1,0:T(8,128)S(1)} %get-tuple-element.34), kind=kOutput, calls=%fused_computation.26 | convolution fusion | flops 3221749760 | bytes 23069184 | tf_op jit(solution)/shard_map/rinj,rnjk->rik/dot_general | solution.py:64
  201.7 10.8 fusion.71
  212.6 13.3 %fusion.12 = f32[32,64,512,1]{2,1,3,0:T(8,128)} fusion(f32[32,4,64,512]{3,2,1,0:T(8,128)S(1)} %bitcast.211, f32[32,64,4,64]{3,2,1,0:T(4,128)S(1)} %copy-done.3, f32[32,4]{1,0:T(8,128)} %get-tuple-element.35), kind=kOutput, calls=%fused_computation.24 | convolution fusion | flops 3221749760 | bytes 23069184 | tf_op jit(solution)/shard_map/rinj,rnjk->rik/dot_general | solution.py:64
  225.8 10.5 fusion.77
  236.4 15.3 %fusion.11 = f32[32,64,512,1]{2,1,3,0:T(8,128)} fusion(f32[32,4,64,512]{3,2,1,0:T(8,128)} %bitcast.208, f32[32,64,4,64]{3,2,1,0:T(4,128)S(1)} %copy-done.2, f32[32,4]{1,0:T(8,128)S(1)} %get-tuple-element.36), kind=kOutput, calls=%fused_computation.22 | convolution fusion | flops 3221749760 | bytes 23069184 | tf_op jit(solution)/shard_map/rinj,rnjk->rik/dot_general | solution.py:64
  251.7 10.4 fusion.83
  262.1 12.6 %fusion.10 = f32[32,64,512,1]{2,1,3,0:T(8,128)} fusion(f32[32,4,64,512]{3,2,1,0:T(8,128)S(1)} %bitcast.207, f32[32,64,4,64]{3,2,1,0:T(4,128)S(1)} %copy-done.1, f32[32,4]{1,0:T(8,128)S(1)} %fusion.111), kind=kOutput, calls=%fused_computation.20 | convolution fusion | flops 3221749760 | bytes 23069184 | tf_op jit(solution)/shard_map/rinj,rnjk->rik/dot_general | solution.py:64
  274.6 10.4 fusion.89
  285.0 7.9 add.113
  293.0 5.9 copy.40
  298.9 840.3 %all-gather.2.cloned.1.call-done = f32[32,5,512,512]{3,2,1,0:T(8,128)} async-done(((f32[1,5,512,512]{3,2,1,0:T(8,128)}), f32[32,5,512,512]{3,2,1,0:T(8,128)}) %all-gather.2.cloned.1.call-update) | async-done | bytes 167772176 | tf_op jit(solution)/shard_map/all_gather | solution.py:80
  1139.2 53.2 %reduce_sum.9 = f32[5,512,512]{2,1,0:T(8,128)} reduce(f32[32,5,512,512]{3,2,1,0:T(8,128)} %all-gather.2.cloned.1.call-done, f32[]{:T(128)} %constant.2.clone.1), dimensions={0}, to_apply=%region_0.0 | reduce | flops 40632320 | bytes 173015040 | tf_op jit(solution)/shard_map/reduce_sum | solution.py:80
  (94 shorter events, 65.1 us)
Async XLA Ops:
  6.5 1132.7 %all-gather.2.cloned.1.call-start = ((), (), s32[]{:S(2)}) async-start(), calls=%async_computation | async-start | bytes 173015040 | tf_op jit(solution)/shard_map/all_gather | solution.py:80
  7.5 71.3 %collective-permute-start.1 = (f32[16,1,512]{2,1,0:T(1,128)S(1)}, f32[16,1,512]{2,1,0:T(1,128)S(1)}, u32[]{:S(2)}, u32[]{:S(2)}) collective-permute-start(f32[16,1,512]{2,1,0:T(1,128)S(1)} %slice.94), channel_id=1, source_target_pairs={{1,0},{2,1},{3,2},{4,3},{5,4},{6,5},{7,6},{9,8},{10,9},{11,10},{12... | collective-permute-start | bytes 98312 | tf_op jit(solution)/shard_map/ppermute | solution.py:12
  9.7 71.8 %collective-permute-start = (f32[1,32,512]{2,1,0:T(8,128)S(1)}, f32[1,32,512]{2,1,0:T(8,128)S(1)}, u32[]{:S(2)}, u32[]{:S(2)}) collective-permute-start(f32[1,32,512]{2,1,0:T(8,128)S(1)} %slice.91), channel_id=1, source_target_pairs={{8,0},{16,8},{24,16},{9,1},{17,9},{25,17},{10,2},{18,10},{26,18},{... | collective-permute-start | bytes 196616 | tf_op jit(solution)/shard_map/ppermute | solution.py:12
  15.4 82.9 %collective-permute-start.5 = (f32[4,64,512]{2,1,0:T(8,128)}, f32[4,64,512]{2,1,0:T(8,128)}, u32[]{:S(2)}, u32[]{:S(2)}) collective-permute-start(f32[4,64,512]{2,1,0:T(8,128)} %gather_fusion.3), channel_id=1, source_target_pairs={{0,7},{1,0},{2,1},{3,2},{4,3},{5,4},{6,5},{7,6},{8,15},{9,8},{10,9... | collective-permute-start | bytes 1572872 | tf_op jit(solution)/shard_map/ppermute | solution.py:18
  20.0 16.5 %copy-start.8 = (s32[5,32]{1,0:T(8,128)S(1)}, s32[5,32]{1,0:T(8,128)}, u32[]{:S(2)}) copy-start(s32[5,32]{1,0:T(8,128)} %param.12) | copy-start | bytes 1924
  20.0 16.5 %copy-start.7 = (s32[5,32,4]{1,2,0:T(4,128)S(1)}, s32[5,32,4]{1,2,0:T(4,128)}, u32[]{:S(2)}) copy-start(s32[5,32,4]{1,2,0:T(4,128)} %param.11) | copy-start | bytes 7684
  20.1 17.6 %copy-start.6 = (f32[5,16,32]{2,1,0:T(8,128)S(1)}, f32[5,16,32]{2,1,0:T(8,128)}, u32[]{:S(2)}) copy-start(f32[5,16,32]{2,1,0:T(8,128)} %param.8) | copy-start | bytes 30724
  20.1 17.6 %copy-start = (f32[16,32,512]{2,1,0:T(8,128)S(1)}, f32[16,32,512]{2,1,0:T(8,128)}, u32[]{:S(2)}) copy-start(f32[16,32,512]{2,1,0:T(8,128)} %param.7) | copy-start | bytes 3145732
  23.7 71.8 %collective-permute-start.3 = (f32[4,64,512]{2,1,0:T(8,128)}, f32[4,64,512]{2,1,0:T(8,128)}, u32[]{:S(2)}, u32[]{:S(2)}) collective-permute-start(f32[4,64,512]{2,1,0:T(8,128)} %gather_fusion.1), channel_id=1, source_target_pairs={{0,24},{8,0},{16,8},{24,16},{1,25},{9,1},{17,9},{25,17},{2,26},{10... | collective-permute-start | bytes 1572872 | tf_op jit(solution)/shard_map/ppermute | solution.py:18
  31.7 62.0 %collective-permute-start.2 = (f32[4,64,512]{2,1,0:T(8,128)}, f32[4,64,512]{2,1,0:T(8,128)}, u32[]{:S(2)}, u32[]{:S(2)}) collective-permute-start(f32[4,64,512]{2,1,0:T(8,128)} %gather_fusion), channel_id=1, source_target_pairs={{0,8},{8,16},{16,24},{24,0},{1,9},{9,17},{17,25},{25,1},{2,10},{10... | collective-permute-start | bytes 1572872 | tf_op jit(solution)/shard_map/ppermute | solution.py:18
  78.8 18.6 %collective-permute-start.4 = (f32[4,64,512]{2,1,0:T(8,128)}, f32[4,64,512]{2,1,0:T(8,128)S(1)}, u32[]{:S(2)}, u32[]{:S(2)}) collective-permute-start(f32[4,64,512]{2,1,0:T(8,128)} %gather_fusion.2), channel_id=1, source_target_pairs={{0,1},{1,2},{2,3},{3,4},{4,5},{5,6},{6,7},{7,0},{8,9},{9,10},{10,1... | collective-permute-start | bytes 1572872 | tf_op jit(solution)/shard_map/ppermute | solution.py:18
  163.8 14.5 %copy-start.5 = (f32[32,64,512]{2,1,0:T(8,128)S(1)}, f32[32,64,512]{2,1,0:T(8,128)}, u32[]{:S(2)}) copy-start(f32[32,64,512]{2,1,0:T(8,128)} %param.9) | copy-start | bytes 12582916
  178.4 8.0 copy-start.4
  186.4 26.1 %slice-start.4 = ((s8[16777216]{0:T(1024)(128)(4,1)}), s8[4194304]{0:T(1024)(128)(4,1)S(1)}, s32[]{:S(2)}) async-start(s8[16777216]{0:T(1024)(128)(4,1)} %bitcast.209), calls=%async_computation.5 | async-start | bytes 8388608
  186.4 26.1 %slice-start.5 = ((s8[16777216]{0:T(1024)(128)(4,1)}), s8[4194304]{0:T(1024)(128)(4,1)S(1)}, s32[]{:S(2)}) async-start(s8[16777216]{0:T(1024)(128)(4,1)} %bitcast.209), calls=%async_computation.6 | async-start | bytes 8388608
  186.4 26.1 %slice-start.6 = ((s8[16777216]{0:T(1024)(128)(4,1)}), s8[4194304]{0:T(1024)(128)(4,1)S(1)}, s32[]{:S(2)}) async-start(s8[16777216]{0:T(1024)(128)(4,1)} %bitcast.209), calls=%async_computation.7 | async-start | bytes 8388608
  201.7 10.9 slice-start.7
  201.7 10.9 copy-start.3
  225.8 10.5 copy-start.2
  236.4 25.7 %slice-start = ((s8[16777216]{0:T(1024)(128)(4,1)}), s8[4194304]{0:T(1024)(128)(4,1)S(1)}, s32[]{:S(2)}) async-start(s8[16777216]{0:T(1024)(128)(4,1)} %bitcast.205), calls=%async_computation.1 | async-start | bytes 8388608
  236.4 25.7 %slice-start.1 = ((s8[16777216]{0:T(1024)(128)(4,1)}), s8[4194304]{0:T(1024)(128)(4,1)S(1)}, s32[]{:S(2)}) async-start(s8[16777216]{0:T(1024)(128)(4,1)} %bitcast.205), calls=%async_computation.2 | async-start | bytes 8388608
  236.4 25.7 %slice-start.2 = ((s8[16777216]{0:T(1024)(128)(4,1)}), s8[4194304]{0:T(1024)(128)(4,1)S(1)}, s32[]{:S(2)}) async-start(s8[16777216]{0:T(1024)(128)(4,1)} %bitcast.205), calls=%async_computation.3 | async-start | bytes 8388608
  251.7 10.4 slice-start.3
  251.7 10.4 copy-start.1
Sparse Core Ops, SparseCore 0:
  299.0 840.0 all-gather.1
